TPU v7x, 32 devices: a whole 2x2x4 slice. The times are simulated.
32 devices in a mesh: parts: 2 (over y), row: 4 (over z), col: 4 (over x, core).
Axes of the slice: x: 2, y: 2, z: 4, core: 2. Of those that a mesh axis runs over, the one named last changes fastest.
Arguments:
- single: bfloat16 [8, 1024, 768], P(None, ('parts', 'row'), 'col'), parts along dimension 1, may hold values from -6 to 6
- pair_act: bfloat16 [1024, 512, 128], P(('parts', 'row'), 'col'), parts along dimension 0, may hold values from -6 to 6
- token_mask: int32 [1024], P(('parts', 'row')), parts along dimension 0, may hold values 0 or 1
- atom_feats: bfloat16 [8192, 128], P(('parts', 'row', 'col')), parts along dimension 0, may hold values from -6 to 6
- atom_token: int32 [8192], P(('parts', 'row', 'col')), parts along dimension 0, may hold values from 0 to 127, as said below
- atom_count: int32 [32], P(('parts', 'row', 'col')), parts along dimension 0, may hold values from 32 to 256, as said below
- atom_weight: bfloat16 [128, 768], P(None, 'col'), may hold values from -0.5 to 0.5
- bias_weight: bfloat16 [128, 2, 16], replicated, may hold values from -16 to 16
- qkvg_weight: bfloat16 [2, 4, 768, 768], P(None, None, 'col'), may hold values from -0.21875 to 0.21875
- out_weight: bfloat16 [2, 768, 768], P(None, 'col'), may hold values from -0.21875 to 0.21875
Outputs:
- updated: bfloat16 [8, 1024, 768], P(None, ('parts', 'row'), 'col'), parts along dimension 1
There are 2 independent parts, one for each index of `parts`. A program takes and returns all parts, laid end to end along the dimension named above; an argument that names none is the same for every part. Nothing has to cross between parts.
Inputs may be any that keep to these rules, and one draw needn't show every extreme that they name: `atom_token`: slots of a device hold atoms of the 128 tokens of that device's row block, numbered within the block; every token owns at least one live slot. The first atom_count slots of a device are live, the others are padding; in every draw some device has all 256 slots live.
All inputs are finite; a program needn't handle non-finite values. No bound on the sum of `token_mask` on one device may be relied on, other than what follows from the above.
Results may differ from a plain program's by a relative error of at most 0.014.
The roundings to bfloat16 on the way count: a program that leaves them out, or rounds other values in their place, can miss the bound.
Values may be sent and summed in bfloat16 or wider, within the bound.
A program may use at most 64 MiB of HBM per device.

v0:
```python
import math
import jax
import jax.numpy as jnp
from jax import lax
from jax.sharding import PartitionSpec as P

HEAD_DIM = 48
LAYERS = 2
EPS = 1e-05
MASKED = -1000000000.0
START_LOW = -1e30


def layer_norm(values):
    average = jnp.mean(values, axis=-1, keepdims=True)
    centered = values - average
    variance = jnp.mean(centered * centered, axis=-1, keepdims=True)
    return centered * lax.rsqrt(variance + EPS)


def per_device(
    single,
    pair_act,
    token_mask,
    atom_feats,
    atom_token,
    atom_count,
    atom_weight,
    bias_weight,
    qkvg_weight,
    out_weight,
):
    tok_rows = single.shape[1]
    sample_count = single.shape[0]
    slot_ids = jnp.arange(atom_feats.shape[0], dtype=jnp.int32)
    live_slots = slot_ids < atom_count[0]
    token_ids = jnp.arange(tok_rows, dtype=jnp.int32)
    owner_match = (token_ids[:, None] == atom_token[None, :]) & live_slots[None, :]
    owners = owner_match.astype(jnp.float32)
    counts = jnp.sum(owners, axis=1)
    atom_sums = jnp.dot(
        owner_match.astype(jnp.bfloat16), atom_feats, preferred_element_type=jnp.float32
    )
    sum_total, count_total = (
        lax.psum(atom_sums.astype(jnp.bfloat16), "col").astype(jnp.float32),
        lax.psum(counts[:, None].astype(jnp.bfloat16), "col").astype(jnp.float32),
    )
    pooled = (
        jnp.dot(sum_total, atom_weight.astype(jnp.float32), precision=lax.Precision.HIGHEST)
        / count_total
    )
    stream = (single.astype(jnp.float32) + pooled[None]).astype(jnp.bfloat16)
    pair_normed = layer_norm(pair_act.astype(jnp.float32)).astype(jnp.bfloat16)
    biases = jnp.einsum(
        "ijc,clh->lhij", pair_normed, bias_weight, preferred_element_type=jnp.float32
    ).astype(jnp.bfloat16)
    live_keys = (token_mask > 0).astype(jnp.bfloat16)[None, :]
    score_scale = 1.0 / math.sqrt(HEAD_DIM)
    for layer_idx in range(LAYERS):
        spread = lax.all_to_all(biases[layer_idx], "col", split_axis=0, concat_axis=2, tiled=True)
        gathered = lax.all_gather(stream, "col", axis=2, tiled=True)
        normed = layer_norm(gathered.astype(jnp.float32)).astype(jnp.bfloat16)
        projected = jnp.einsum(
            "std,fed->fste", normed, qkvg_weight[layer_idx], preferred_element_type=jnp.float32
        )
        head_width = projected.shape[3]
        heads_here = head_width // HEAD_DIM
        queries = (
            projected[0].astype(jnp.bfloat16).reshape(sample_count, tok_rows, heads_here, HEAD_DIM)
        )
        key_rows = projected[1].astype(jnp.bfloat16)
        value_rows = projected[2].astype(jnp.bfloat16)
        gating = jax.nn.sigmoid(projected[3])

        def attend(running, incoming, offset, queries=queries, spread=spread):
            top_old, summed_old, acc_old = running
            keys_in, values_in, live_in = incoming
            key_count = keys_in.shape[1]
            keys_heads = keys_in.reshape(sample_count, key_count, heads_here, HEAD_DIM)
            values_heads = values_in.reshape(sample_count, key_count, heads_here, HEAD_DIM)
            scores = (
                jnp.einsum(
                    "sqhd,skhd->shqk", queries, keys_heads, preferred_element_type=jnp.float32
                )
                * score_scale
            )
            scores = scores + spread.astype(jnp.float32)[None]
            scores = jnp.where(live_in[0][None, None, None, :] > 0, scores, MASKED)
            top_new = jnp.maximum(top_old, jnp.max(scores, axis=-1))
            exponent = jnp.exp(scores - top_new[..., None])
            summed_new = jnp.sum(exponent, axis=-1)
            weights = exponent.astype(jnp.bfloat16)
            acc_new = jnp.einsum(
                "shqk,skhd->shqd", weights, values_heads, preferred_element_type=jnp.float32
            )
            return (top_new, summed_new, acc_new)

        start_state = (
            jnp.full((sample_count, heads_here, tok_rows), START_LOW, jnp.float32),
            jnp.zeros((sample_count, heads_here, tok_rows), jnp.float32),
            jnp.zeros((sample_count, heads_here, tok_rows, HEAD_DIM), jnp.float32),
        )
        top_end, summed_end, acc_end = attend(
            start_state,
            (
                lax.all_gather(key_rows, "row", axis=1, tiled=True),
                lax.all_gather(value_rows, "row", axis=1, tiled=True),
                lax.all_gather(live_keys, "row", axis=1, tiled=True),
            ),
            jnp.int32(0),
        )
        attended = acc_end / summed_end[..., None]
        attended = attended.transpose(0, 2, 1, 3).reshape(sample_count, tok_rows, head_width)
        gated = (gating * attended).astype(jnp.bfloat16)
        out_rows = out_weight[layer_idx]

        def project(summed, incoming, offset, out_rows=out_rows):
            return jnp.einsum("std,ed->ste", incoming, out_rows, preferred_element_type=jnp.float32)

        zero_update = jnp.zeros((sample_count, tok_rows, out_rows.shape[0]), jnp.float32)
        update = project(
            zero_update, lax.all_gather(gated, "col", axis=2, tiled=True), jnp.int32(0)
        )
        stream = (stream.astype(jnp.float32) + update).astype(jnp.bfloat16)
    return stream


def solution(mesh):
    placed = (
        P(None, ("parts", "row"), "col"),
        P(("parts", "row"), "col", None),
        P(("parts", "row")),
        P(("parts", "row", "col"), None),
        P(("parts", "row", "col")),
        P(("parts", "row", "col")),
        P(None, "col"),
        P(),
        P(None, None, "col", None),
        P(None, "col", None),
    )
    return jax.shard_map(
        per_device,
        mesh=mesh,
        in_specs=placed,
        out_specs=P(None, ("parts", "row"), "col"),
        check_vma=False,
    )
```

profile of v0, /device:TPU:0, one launch (start us, length us, event | category | flops | bytes accessed | tf_op | source)
XLA Modules:
  0.0 297.7 jit_solution(7858886814213033118)
XLA Ops:
  7.4 0.8 convert_reduce_fusion.3
  8.2 0.8 convolution_convert_fusion
  9.0 13.2 %all-reduce = (bf16[128,128]{1,0:T(8,128)(2,1)S(1)}, bf16[128]{0:T(256)(128)(2,1)S(1)}) all-reduce(bf16[128,128]{1,0:T(8,128)(2,1)S(1)} %convolution_convert_fusion, bf16[128]{0:T(256)(128)(2,1)S(1)} %convert_reduce_fusion.3), channel_id=1, replica_groups=mesh['parts'=2,'row'=4,'col'=4] {'col'}, use_global_device_ids=true, to_apply=%region_0.0 | all-reduce | flops 16512 | bytes 66048 | tf_op jit(solution)/shard_map/psum | solution.py:45
  22.2 1.0 convolution_divide_fusion
  23.1 1.8 add_convert_fusion
  25.0 0.0 all-gather.23.cloned.1.call-start
  25.0 20.1 %all-gather.15.cloned.1.call-done = bf16[8,128,768]{1,2,0:T(8,128)(2,1)} async-done(((bf16[8,128,192]{1,2,0:T(8,128)(2,1)}), bf16[8,128,768]{1,2,0:T(8,128)(2,1)}) %all-gather.15.cloned.1.call-update) | async-done | bytes 1572880 | tf_op jit(solution)/shard_map/all_gather | solution.py:61
  45.1 1.7 convert_reduce_fusion.2
  46.8 1.8 fusion.25
  48.7 3.2 %fusion.87 = (bf16[4,8,128,192]{2,3,0,1:T(8,128)(2,1)S(1)}, f32[4,8,128,192]{2,3,0,1:T(8,128)}) fusion(bf16[2,4,192,768]{3,2,1,0:T(8,128)(2,1)S(1)} %copy-done.9, bf16[8,128,768]{1,2,0:T(8,128)(2,1)S(1)} %copy-done.4, f32[8,128]{1,0:T(8,128)S(1)} %add_rsqrt_fusion.2, f32[8,128]{1,0:T(8,128)S(1)} %broadcast_multiply_fusion.2), kind=kOutput, calls=%fused_computation.107 | convolution fusion | flops 1211891712 | bytes 7479296 | tf_op jit(solution)/shard_map/std,fed->fste/dot_general | solution.py:63
  51.9 1.0 fusion.86
  53.0 3.5 %convert_reduce_fusion = f32[128,128]{1,0:T(8,128)S(1)} fusion(bf16[128,128,128]{2,1,0:T(8,128)(2,1)} %param.11), kind=kLoop, calls=%fused_computation.1 | loop fusion | flops 4177920 | bytes 4259840 | tf_op jit(solution)/shard_map/reduce_sum | solution.py:15
  56.5 4.8 %fusion.2 = f32[128,128]{1,0:T(8,128)S(1)} fusion(bf16[128,128,128]{2,1,0:T(8,128)(2,1)S(1)} %copy-done.3, f32[128,128]{1,0:T(8,128)S(1)} %broadcast_multiply_fusion), kind=kLoop, calls=%fused_computation.4 | loop fusion | flops 8372224 | bytes 4325376 | tf_op jit(solution)/shard_map/reduce_sum | solution.py:17
  61.4 6.0 %fusion.38 = bf16[2,16,128,128]{3,1,0,2:T(8,128)(2,1)S(1)} fusion(bf16[128,128,128]{2,1,0:T(8,128)(2,1)S(1)} %copy-done.3, f32[128,128]{1,0:T(8,128)S(1)} %add_rsqrt_fusion, f32[128,128]{1,0:T(8,128)S(1)} %broadcast_multiply_fusion, bf16[128,2,16]{0,2,1:T(8,128)(2,1)S(1)} %copy-done.10), kind=kOutput, calls=%fused_computation.43 | convolution fusion | flops 143130624 | bytes 5382144 | tf_op jit(solution)/shard_map/ijc,clh->lhij/dot_general | solution.py:54
  67.4 0.2 slice_bitcast_fusion
  67.6 0.9 copy.26
  68.5 3.5 %all-to-all-start = ((bf16[16,128,128]{2,1,0:T(8,128)(2,1)}), bf16[16,128,128]{2,1,0:T(8,128)(2,1)S(1)}, u32[]{:S(2)}, u32[]{:S(2)}) async-start(bf16[16,128,128]{2,1,0:T(8,128)(2,1)} %copy.26), calls=%async_computation | async-start | bytes 1048576 | tf_op jit(solution)/shard_map/all_to_all | solution.py:60
  72.0 0.0 all-gather.17.cloned.1.call-start
  72.0 12.2 %all-gather.5 = bf16[4,1,128]{2,1,0:T(2,128)(2,1)S(1)} all-gather(bf16[1,1,128]{2,1,0:T(2,128)(2,1)S(1)} %fusion.80), channel_id=2, replica_groups=mesh['parts'=2,'row'=4,'col'=4] {'row'}, dimensions={0}, use_global_device_ids=true | all-gather | bytes 1280 | tf_op jit(solution)/shard_map/all_gather | solution.py:108
  84.3 0.1 copy_bitcast_fusion.1
  84.4 6.4 %all-gather.23.cloned.1.call-done = bf16[1,8,512,192]{2,3,0,1:T(8,128)(2,1)} async-done(((bf16[1,8,128,192]{2,3,0,1:T(8,128)(2,1)}), bf16[1,8,512,192]{2,3,0,1:T(8,128)(2,1)}) %all-gather.23.cloned.1.call-update) | async-done | bytes 1572880 | tf_op jit(solution)/shard_map/all_gather | solution.py:106
  90.8 3.3 %fusion.8 = (f32[8,4,128]{2,1,0:T(4,128)S(1)}, f32[8,4,128,512]{3,2,1,0:T(8,128)S(1)}) fusion(f32[4,128,512]{2,1,0:T(8,128)S(1)} %copy_bitcast_fusion.1, pred[512]{0:T(512)(128)(4,1)S(1)} %bitcast.132, bf16[8,128,4,48]{1,3,2,0:T(8,128)(2,1)S(1)} %bitcast.126, bf16[8,512,4,48]{1,3,2,0:T(8,128)(2,1)} %bitcast.128), kind=kOutput, calls=%fused_computation.14 | convolution fusion | flops 209711104 | bytes 11420160 | tf_op jit(solution)/shard_map/sqhd,skhd->shqk/dot_general | solution.py:82
  94.1 3.2 %copy-done.2 = f32[8,4,128,512]{3,2,1,0:T(8,128)} copy-done((f32[8,4,128,512]{3,2,1,0:T(8,128)}, f32[8,4,128,512]{3,2,1,0:T(8,128)S(1)}, u32[]{:S(2)}) %copy-start.2) | copy-done | bytes 8388632
  97.3 2.3 fusion.4
  99.7 28.6 %all-gather.25.cloned.1.call-done = bf16[1,8,512,192]{2,3,0,1:T(8,128)(2,1)} async-done(((bf16[1,8,128,192]{2,3,0,1:T(8,128)(2,1)}), bf16[1,8,512,192]{2,3,0,1:T(8,128)(2,1)}) %all-gather.25.cloned.1.call-update) | async-done | bytes 1572880 | tf_op jit(solution)/shard_map/all_gather | solution.py:107
  128.3 6.3 %fusion.56 = f32[8,128,4,48]{1,3,2,0:T(8,128)S(1)} fusion(bf16[8,512,4,48]{1,3,2,0:T(8,128)(2,1)} %bitcast.138, f32[8,4,128,512]{3,2,1,0:T(8,128)} %copy-done.2, f32[8,4,128]{2,1,0:T(4,128)S(1)} %broadcast_maximum_fusion.1, f32[4,128,512]{2,1,0:T(8,128)S(1)} %copy_bitcast_fusion.1, pred[512]{0:T(512)(128)(4,1)S(1)} %bitcast.134, f32[8,128,4]{1,2,0:T(4,128)S(1)} %bitcast.131), kind=kOutput, calls=%fused_computation.61 | convolution fusion | flops 212008960 | bytes 11829760 | tf_op jit(solution)/shard_map/shqk,skhd->shqd/dot_general | solution.py:93
  134.6 2.2 fusion.69
  136.8 0.0 all-gather.19.cloned.1.call-start
  136.8 18.0 %all-gather.17.cloned.1.call-done = bf16[8,128,768]{1,2,0:T(8,128)(2,1)} async-done(((bf16[8,128,192]{1,2,0:T(8,128)(2,1)}), bf16[8,128,768]{1,2,0:T(8,128)(2,1)}) %all-gather.17.cloned.1.call-update) | async-done | bytes 1572880 | tf_op jit(solution)/shard_map/all_gather | solution.py:122
  154.8 2.6 fusion.47
  157.5 19.7 %all-gather.19.cloned.1.call-done = bf16[8,128,768]{1,2,0:T(8,128)(2,1)} async-done(((bf16[8,128,192]{1,2,0:T(8,128)(2,1)}), bf16[8,128,768]{1,2,0:T(8,128)(2,1)}) %all-gather.19.cloned.1.call-update) | async-done | bytes 1572880 | tf_op jit(solution)/shard_map/all_gather | solution.py:61
  177.3 1.7 convert_reduce_fusion.1
  179.0 1.8 fusion.23
  180.9 4.5 %fusion.88 = (bf16[4,8,128,192]{2,3,0,1:T(8,128)(2,1)S(1)}, f32[4,8,128,192]{2,3,0,1:T(8,128)}) fusion(bf16[2,4,192,768]{3,2,1,0:T(8,128)(2,1)} %param.18, bf16[8,128,768]{1,2,0:T(8,128)(2,1)S(1)} %copy-done.5, f32[8,128]{1,0:T(8,128)S(1)} %add_rsqrt_fusion.1, f32[8,128]{1,0:T(8,128)S(1)} %broadcast_multiply_fusion.1), kind=kOutput, calls=%fused_computation.108 | convolution fusion | flops 1211891712 | bytes 7479296 | tf_op jit(solution)/shard_map/std,fed->fste/dot_general | solution.py:63
  185.3 1.0 fusion.85
  186.4 0.7 all-gather.29.cloned.1.call-update
  187.2 0.1 copy.29
  187.3 11.2 %all_to_all.8 = bf16[16,128,128]{2,1,0:T(8,128)(2,1)S(1)} all-to-all(bf16[16,128,128]{2,1,0:T(8,128)(2,1)S(1)} %copy.29), channel_id=1, replica_groups=mesh['parts'=2,'row'=4,'col'=4] {'col'}, dimensions={0} | all-to-all | bytes 1048576 | tf_op jit(solution)/shard_map/all_to_all | solution.py:60
  198.5 0.1 copy_bitcast_fusion
  198.7 25.6 %all-gather.27.cloned.1.call-done = bf16[1,8,512,192]{2,3,0,1:T(8,128)(2,1)} async-done(((bf16[1,8,128,192]{2,3,0,1:T(8,128)(2,1)}), bf16[1,8,512,192]{2,3,0,1:T(8,128)(2,1)}) %all-gather.27.cloned.1.call-update) | async-done | bytes 1572880 | tf_op jit(solution)/shard_map/all_gather | solution.py:106
  224.2 3.3 %fusion.9 = (f32[8,4,128]{2,1,0:T(4,128)S(1)}, f32[8,4,128,512]{3,2,1,0:T(8,128)S(1)}) fusion(f32[4,128,512]{2,1,0:T(8,128)S(1)} %copy_bitcast_fusion, pred[512]{0:T(512)(128)(4,1)S(1)} %bitcast.135, bf16[8,128,4,48]{1,3,2,0:T(8,128)(2,1)S(1)} %bitcast.127, bf16[8,512,4,48]{1,3,2,0:T(8,128)(2,1)} %bitcast.129), kind=kOutput, calls=%fused_computation.15 | convolution fusion | flops 209711104 | bytes 11420160 | tf_op jit(solution)/shard_map/sqhd,skhd->shqk/dot_general | solution.py:82
  227.5 3.2 %copy-done.1 = f32[8,4,128,512]{3,2,1,0:T(8,128)} copy-done((f32[8,4,128,512]{3,2,1,0:T(8,128)}, f32[8,4,128,512]{3,2,1,0:T(8,128)S(1)}, u32[]{:S(2)}) %copy-start.1) | copy-done | bytes 8388632
  230.7 2.3 fusion.6
  233.1 28.6 %all-gather.29.cloned.1.call-done = bf16[1,8,512,192]{2,3,0,1:T(8,128)(2,1)} async-done(((bf16[1,8,128,192]{2,3,0,1:T(8,128)(2,1)}), bf16[1,8,512,192]{2,3,0,1:T(8,128)(2,1)}) %all-gather.29.cloned.1.call-update) | async-done | bytes 1572880 | tf_op jit(solution)/shard_map/all_gather | solution.py:107
  261.7 6.3 %fusion.53 = f32[8,128,4,48]{1,3,2,0:T(8,128)S(1)} fusion(bf16[8,512,4,48]{1,3,2,0:T(8,128)(2,1)} %bitcast.139, f32[8,4,128,512]{3,2,1,0:T(8,128)} %copy-done.1, f32[8,4,128]{2,1,0:T(4,128)S(1)} %broadcast_maximum_fusion, f32[4,128,512]{2,1,0:T(8,128)S(1)} %copy_bitcast_fusion, pred[512]{0:T(512)(128)(4,1)S(1)} %bitcast.137, f32[8,128,4]{1,2,0:T(4,128)S(1)} %bitcast.130), kind=kOutput, calls=%fused_computation.60 | convolution fusion | flops 212008960 | bytes 11829760 | tf_op jit(solution)/shard_map/shqk,skhd->shqd/dot_general | solution.py:93
  268.0 2.2 fusion.70
  270.2 18.0 %all-gather.21.cloned.1.call-done = bf16[8,128,768]{1,2,0:T(8,128)(2,1)} async-done(((bf16[8,128,192]{1,2,0:T(8,128)(2,1)}), bf16[8,128,768]{1,2,0:T(8,128)(2,1)}) %all-gather.21.cloned.1.call-update) | async-done | bytes 1572880 | tf_op jit(solution)/shard_map/all_gather | solution.py:122
  288.2 2.6 fusion.48
  (47 shorter events, 0.4 us)
Async XLA Ops:
  6.5 1.6 copy-start
  6.5 42.2 %copy-start.9 = (bf16[2,4,192,768]{3,2,1,0:T(8,128)(2,1)S(1)}, bf16[2,4,192,768]{3,2,1,0:T(8,128)(2,1)}, u32[]{:S(2)}) copy-start(bf16[2,4,192,768]{3,2,1,0:T(8,128)(2,1)} %param.18) | copy-start | bytes 7077892
  6.5 38.6 %all-gather.15.cloned.1.call-start = ((), (), s32[]{:S(2)}) async-start(), calls=%async_computation.2 | async-start | bytes 1966080 | tf_op jit(solution)/shard_map/all_gather | solution.py:61
  25.0 65.8 %all-gather.23.cloned.1.call-start = ((), (), s32[]{:S(2)}) async-start(), calls=%async_computation.6 | async-start | bytes 1966080 | tf_op jit(solution)/shard_map/all_gather | solution.py:106
  45.1 3.6 %copy-start.4 = (bf16[8,128,768]{1,2,0:T(8,128)(2,1)S(1)}, bf16[8,128,768]{1,2,0:T(8,128)(2,1)}, u32[]{:S(2)}) copy-start(bf16[8,128,768]{1,2,0:T(8,128)(2,1)} %all-gather.15.cloned.1.call-done) | copy-start | bytes 4718596
  52.9 75.3 %all-gather.25.cloned.1.call-start = ((), (), s32[]{:S(2)}) async-start(), calls=%async_computation.7 | async-start | bytes 1966080 | tf_op jit(solution)/shard_map/all_gather | solution.py:107
  53.0 3.6 %copy-start.3 = (bf16[128,128,128]{2,1,0:T(8,128)(2,1)S(1)}, bf16[128,128,128]{2,1,0:T(8,128)(2,1)}, u32[]{:S(2)}) copy-start(bf16[128,128,128]{2,1,0:T(8,128)(2,1)} %param.11) | copy-start | bytes 12582916
  56.5 4.8 %copy-start.10 = (bf16[128,2,16]{0,2,1:T(8,128)(2,1)S(1)}, bf16[128,2,16]{0,2,1:T(8,128)(2,1)}, u32[]{:S(2)}) copy-start(bf16[128,2,16]{0,2,1:T(8,128)(2,1)} %param.17) | copy-start | bytes 24580
  67.3 4.7 %copy-start.11 = (s32[128]{0:T(128)S(1)}, s32[128]{0:T(128)}, u32[]{:S(2)}) copy-start(s32[128]{0:T(128)} %param.12) | copy-start | bytes 1540
  68.5 15.8 %all-to-all-start = ((bf16[16,128,128]{2,1,0:T(8,128)(2,1)}), bf16[16,128,128]{2,1,0:T(8,128)(2,1)S(1)}, u32[]{:S(2)}, u32[]{:S(2)}) async-start(bf16[16,128,128]{2,1,0:T(8,128)(2,1)} %copy.26), calls=%async_computation | async-start | bytes 1048576 | tf_op jit(solution)/shard_map/all_to_all | solution.py:60
  72.0 82.8 %all-gather.17.cloned.1.call-start = ((), (), s32[]{:S(2)}) async-start(), calls=%async_computation.3 | async-start | bytes 1966080 | tf_op jit(solution)/shard_map/all_gather | solution.py:122
  94.1 3.2 %copy-start.2 = (f32[8,4,128,512]{3,2,1,0:T(8,128)}, f32[8,4,128,512]{3,2,1,0:T(8,128)S(1)}, u32[]{:S(2)}) copy-start(f32[8,4,128,512]{3,2,1,0:T(8,128)S(1)} %get-tuple-element.18) | copy-start | bytes 25165828
  128.3 26.5 %copy-start.6 = (bf16[8,128,192]{1,2,0:T(8,128)(2,1)S(1)}, bf16[8,128,192]{1,2,0:T(8,128)(2,1)}, u32[]{:S(2)}) copy-start(bf16[8,128,192]{1,2,0:T(8,128)(2,1)} %add_convert_fusion) | copy-start | bytes 1179652
  128.3 26.5 %copy-start.8 = (bf16[2,192,768]{2,1,0:T(8,128)(2,1)S(1)}, bf16[2,192,768]{2,1,0:T(8,128)(2,1)}, u32[]{:S(2)}) copy-start(bf16[2,192,768]{2,1,0:T(8,128)(2,1)} %param.19) | copy-start | bytes 1769476
  136.8 40.5 %all-gather.19.cloned.1.call-start = ((), (), s32[]{:S(2)}) async-start(), calls=%async_computation.4 | async-start | bytes 1966080 | tf_op jit(solution)/shard_map/all_gather | solution.py:61
  157.5 66.7 %all-gather.27.cloned.1.call-start = ((), (), s32[]{:S(2)}) async-start(), calls=%async_computation.8 | async-start | bytes 1966080 | tf_op jit(solution)/shard_map/all_gather | solution.py:106
  177.3 3.6 %copy-start.5 = (bf16[8,128,768]{1,2,0:T(8,128)(2,1)S(1)}, bf16[8,128,768]{1,2,0:T(8,128)(2,1)}, u32[]{:S(2)}) copy-start(bf16[8,128,768]{1,2,0:T(8,128)(2,1)} %all-gather.19.cloned.1.call-done) | copy-start | bytes 4718596
  186.4 75.3 %all-gather.29.cloned.1.call-start = ((), (), s32[]{:S(2)}) async-start(), calls=%async_computation.9 | async-start | bytes 1966080 | tf_op jit(solution)/shard_map/all_gather | solution.py:107
  187.1 101.1 %all-gather.21.cloned.1.call-start = ((), (), s32[]{:S(2)}) async-start(), calls=%async_computation.5 | async-start | bytes 1966080 | tf_op jit(solution)/shard_map/all_gather | solution.py:122
  227.5 3.2 %copy-start.1 = (f32[8,4,128,512]{3,2,1,0:T(8,128)}, f32[8,4,128,512]{3,2,1,0:T(8,128)S(1)}, u32[]{:S(2)}) copy-start(f32[8,4,128,512]{3,2,1,0:T(8,128)S(1)} %get-tuple-element.22) | copy-start | bytes 25165828
  261.7 26.5 %copy-start.7 = (bf16[8,128,192]{1,2,0:T(8,128)(2,1)S(1)}, bf16[8,128,192]{1,2,0:T(8,128)(2,1)}, u32[]{:S(2)}) copy-start(bf16[8,128,192]{1,2,0:T(8,128)(2,1)} %fusion.47) | copy-start | bytes 1179652
Sparse Core Ops, SparseCore 0:
  25.1 19.9 all-gather.14
  53.0 37.7 all-gather.22
  92.4 35.8 all-gather.24
  136.9 17.8 all-gather.16
  157.6 19.6 all-gather.18
  186.5 37.6 all-gather.26
  225.8 35.9 all-gather.28
  270.3 17.8 all-gather.20
where the time goes:
time: 298 us
  waiting for transfers between devices  166 us (56%)
  matrix products  39.9 us (13%)
  blocking collectives  36.6 us (12%)
  other arithmetic  27.3 us (9%)
  between operations  14.6 us (5%)
  local copies, waits for them, and re-layouts  9.73 us (3%)
  starting transfers between devices  3.76 us (1%)
    all_gather x2, waiting for transfers between devices, per_device(): lax.all_gather(value_rows, 'row', axis=1, tiled=True)  57.2 us
    all_gather x2, waiting for transfers between devices, per_device(): gathered = lax.all_gather(stream, 'col', axis=2, tiled=True)  39.8 us
    all_gather x2, waiting for transfers between devices, per_device(): lax.all_gather(gated, 'col', axis=2, tiled=True)  36 us
    all_gather x2, waiting for transfers between devices, per_device(): lax.all_gather(key_rows, 'row', axis=1, tiled=True)  31.9 us
    psum x1, blocking collectives, per_device(): lax.psum(atom_sums.astype(jnp.bfloat16), 'col').astype(jnp.float32)  13.2 us
    dot_general x2, matrix products, attend(): jnp.einsum('shqk,skhd->shqd', weights, values_heads, preferred_element_ty...  12.6 us
    all_gather x1, blocking collectives, per_device(): lax.all_gather(live_keys, 'row', axis=1, tiled=True)  12.2 us
    all_to_all x1, blocking collectives, per_device(): lax.all_to_all(biases[layer_idx], 'col', split_axis=0, concat_axis=2, til...  11.2 us
  transfers between devices with their start and end apart: 9, of which 8 were waited for; matrix products, arithmetic and copies ran while one was open for 9% of the time, Pallas kernels for 0%

commit v1 on v0

--- a/solution.py
+++ b/solution.py
@@ -9,6 +9,16 @@
 EPS = 1e-05
 MASKED = -1000000000.0
 START_LOW = -1e30
+
+
+def ring_gather(x, axis, dim):
+    ways, here, step = (lax.axis_size(axis), lax.axis_index(axis), x.shape[dim])
+    dims = [n * ways if d == dim else n for d, n in enumerate(x.shape)]
+    full = lax.dynamic_update_slice_in_dim(jnp.zeros(dims, x.dtype), x, here * step, axis=dim)
+    for far in range(1, ways):
+        x = lax.ppermute(x, axis, [(d, (d + 1) % ways) for d in range(ways)])
+        full = lax.dynamic_update_slice_in_dim(full, x, (here - far) % ways * step, axis=dim)
+    return full
 
 
 def layer_norm(values):
@@ -103,7 +113,7 @@
         top_end, summed_end, acc_end = attend(
             start_state,
             (
-                lax.all_gather(key_rows, "row", axis=1, tiled=True),
+                ring_gather(key_rows, "row", 1),
                 lax.all_gather(value_rows, "row", axis=1, tiled=True),
                 lax.all_gather(live_keys, "row", axis=1, tiled=True),
             ),

time: 298 us -> 274 us (0.919)
  waiting for transfers between devices: 166 us -> 140 us
  blocking collectives: 36.6 us -> 27.9 us
  starting transfers between devices: 3.76 us -> 11.6 us
  local copies, waits for them, and re-layouts: 9.73 us -> 14.6 us
    ppermute x0 -> x6, waiting for transfers between devices: none -> 49.5 us  [ring_gather(): x = lax.ppermute(x, axis, [(d, (d + 1) % ways) for d in range(ways)])]
    all_gather x2, waiting for transfers between devices: 57.2 us -> 21.6 us  [per_device(): lax.all_gather(value_rows, 'row', axis=1, tiled=True)]
    all_gather x2 -> x0, waiting for transfers between devices: 31.9 us -> none  [per_device(): lax.all_gather(key_rows, 'row', axis=1, tiled=True)]
    all_to_all x1 -> x0, blocking collectives: 11.2 us -> none  [per_device(): lax.all_to_all(biases[layer_idx], 'col', split_axis=0, concat_axis=2, til...]
    all_gather x2, waiting for transfers between devices: 39.8 us -> 31.5 us  [per_device(): gathered = lax.all_gather(stream, 'col', axis=2, tiled=True)]
    ppermute x0 -> x6, starting transfers between devices: none -> 4.47 us  [ring_gather(): x = lax.ppermute(x, axis, [(d, (d + 1) % ways) for d in range(ways)])]
    all_to_all x1 -> x2, starting transfers between devices: 3.47 us -> 6.94 us  [per_device(): lax.all_to_all(biases[layer_idx], 'col', split_axis=0, concat_axis=2, til...]
    unnamed x24 -> x30, local copies, waits for them, and re-layouts: 6.48 us -> 7.62 us
  transfers between devices with their start and end apart: 9 -> 14, of which waited for: 8 -> 12; matrix products, arithmetic and copies ran while one was open for 9% -> 10% of each run, Pallas kernels for 0% -> 0%
where the time goes in v1:
time: 274 us
  waiting for transfers between devices  140 us (51%)
  matrix products  37.1 us (14%)
  blocking collectives  27.9 us (10%)
  other arithmetic  27.3 us (10%)
  local copies, waits for them, and re-layouts  14.6 us (5%)
  between operations  14.6 us (5%)
  starting transfers between devices  11.6 us (4%)
    ppermute x6, waiting for transfers between devices, ring_gather(): x = lax.ppermute(x, axis, [(d, (d + 1) % ways) for d in range(ways)])  49.5 us
    all_gather x2, waiting for transfers between devices, per_device(): lax.all_gather(gated, 'col', axis=2, tiled=True)  36.1 us
    all_gather x2, waiting for transfers between devices, per_device(): gathered = lax.all_gather(stream, 'col', axis=2, tiled=True)  31.5 us
    all_gather x2, waiting for transfers between devices, per_device(): lax.all_gather(value_rows, 'row', axis=1, tiled=True)  21.6 us
    all_gather x1, blocking collectives, per_device(): lax.all_gather(live_keys, 'row', axis=1, tiled=True)  14.7 us
    psum x1, blocking collectives, per_device(): lax.psum(atom_sums.astype(jnp.bfloat16), 'col').astype(jnp.float32)  13.2 us
    dot_general x2, matrix products, attend(): jnp.einsum('shqk,skhd->shqd', weights, values_heads, preferred_element_ty...  12.6 us
    reduce_sum x3, other arithmetic, layer_norm(): variance = jnp.mean(centered * centered, axis=-1, keepdims=True)  8.43 us
  transfers between devices with their start and end apart: 14, of which 12 were waited for; matrix products, arithmetic and copies ran while one was open for 10% of the time, Pallas kernels for 0%

profile of v1, /device:TPU:0, one launch (start us, length us, event | category | flops | bytes accessed | tf_op | source)
XLA Modules:
  0.0 273.5 jit_solution(13897375159172938435)
XLA Ops:
  8.9 13.2 %all-reduce = (bf16[128,128]{1,0:T(8,128)(2,1)S(1)}, bf16[128]{0:T(256)(128)(2,1)S(1)}) all-reduce(bf16[128,128]{1,0:T(8,128)(2,1)S(1)} %convolution_convert_fusion, bf16[128]{0:T(256)(128)(2,1)S(1)} %convert_reduce_fusion.3), channel_id=1, replica_groups=mesh['parts'=2,'row'=4,'col'=4] {'col'}, use_global_device_ids=true, to_apply=%region_0.0 | all-reduce | flops 16512 | bytes 66048 | tf_op jit(solution)/shard_map/psum | solution.py:55
  22.1 1.0 convolution_divide_fusion
  23.0 1.8 add_convert_fusion
  24.9 3.5 %convert_reduce_fusion = f32[128,128]{1,0:T(8,128)S(1)} fusion(bf16[128,128,128]{2,1,0:T(8,128)(2,1)} %param.11), kind=kLoop, calls=%fused_computation.1 | loop fusion | flops 4177920 | bytes 4259840 | tf_op jit(solution)/shard_map/reduce_sum | solution.py:25
  28.4 4.8 %fusion.2 = f32[128,128]{1,0:T(8,128)S(1)} fusion(bf16[128,128,128]{2,1,0:T(8,128)(2,1)S(1)} %copy-done.3, f32[128,128]{1,0:T(8,128)S(1)} %broadcast_multiply_fusion), kind=kLoop, calls=%fused_computation.4 | loop fusion | flops 8372224 | bytes 4325376 | tf_op jit(solution)/shard_map/reduce_sum | solution.py:27
  33.2 11.7 %all-gather.11.cloned.1.call-done = bf16[8,128,768]{1,2,0:T(8,128)(2,1)} async-done(((bf16[8,128,192]{1,2,0:T(8,128)(2,1)}), bf16[8,128,768]{1,2,0:T(8,128)(2,1)}) %all-gather.11.cloned.1.call-update) | async-done | bytes 1572880 | tf_op jit(solution)/shard_map/all_gather | solution.py:71
  45.0 1.7 convert_reduce_fusion.2
  46.7 1.8 fusion.25
  48.6 3.2 %fusion.85 = (bf16[4,8,128,192]{2,3,0,1:T(8,128)(2,1)S(1)}, f32[4,8,128,192]{2,3,0,1:T(8,128)}) fusion(bf16[2,4,192,768]{3,2,1,0:T(8,128)(2,1)S(1)} %copy-done.12, bf16[8,128,768]{1,2,0:T(8,128)(2,1)S(1)} %copy-done.5, f32[8,128]{1,0:T(8,128)S(1)} %add_rsqrt_fusion.2, f32[8,128]{1,0:T(8,128)S(1)} %broadcast_multiply_fusion.2), kind=kOutput, calls=%fused_computation.115 | convolution fusion | flops 1211891712 | bytes 7479296 | tf_op jit(solution)/shard_map/std,fed->fste/dot_general | solution.py:73
  51.8 1.0 slice_bitcast_fusion.3
  52.7 1.5 collective-permute-start
  54.2 6.0 %fusion.38 = bf16[2,16,128,128]{3,1,0,2:T(8,128)(2,1)S(1)} fusion(bf16[128,128,128]{2,1,0:T(8,128)(2,1)S(1)} %copy-done.4, f32[128,128]{1,0:T(8,128)S(1)} %add_rsqrt_fusion, f32[128,128]{1,0:T(8,128)S(1)} %broadcast_multiply_fusion, bf16[128,2,16]{0,2,1:T(8,128)(2,1)S(1)} %copy-done.13), kind=kOutput, calls=%fused_computation.43 | convolution fusion | flops 143130624 | bytes 5382144 | tf_op jit(solution)/shard_map/ijc,clh->lhij/dot_general | solution.py:64
  60.4 0.9 copy.26
  61.4 3.5 %all-to-all-start = ((bf16[16,128,128]{2,1,0:T(8,128)(2,1)}), bf16[16,128,128]{2,1,0:T(8,128)(2,1)S(1)}, u32[]{:S(2)}, u32[]{:S(2)}) async-start(bf16[16,128,128]{2,1,0:T(8,128)(2,1)} %copy.26), calls=%async_computation | async-start | bytes 1048576 | tf_op jit(solution)/shard_map/all_to_all | solution.py:70
  64.9 0.9 collective-permute-done
  66.4 14.7 %all-gather.3 = bf16[4,1,128]{2,1,0:T(2,128)(2,1)S(1)} all-gather(bf16[1,1,128]{2,1,0:T(2,128)(2,1)S(1)} %fusion.80), channel_id=2, replica_groups=mesh['parts'=2,'row'=4,'col'=4] {'row'}, dimensions={0}, use_global_device_ids=true | all-gather | bytes 1280 | tf_op jit(solution)/shard_map/all_gather | solution.py:118
  81.5 0.9 collective-permute-start.2
  82.5 1.1 constant_dynamic-update-slice_fusion.7
  83.8 11.1 %collective-permute-done.2 = bf16[8,128,192]{1,2,0:T(8,128)(2,1)S(1)} collective-permute-done((bf16[8,128,192]{1,2,0:T(8,128)(2,1)S(1)}, bf16[8,128,192]{1,2,0:T(8,128)(2,1)S(1)}, u32[]{:S(2)}, u32[]{:S(2)}) %collective-permute-start.2) | collective-permute-done | bytes 393248 | tf_op jit(solution)/shard_map/ppermute | solution.py:19
  95.0 1.9 fusion.8
  96.9 3.2 %copy-done.2 = f32[8,4,128,512]{3,2,1,0:T(8,128)} copy-done((f32[8,4,128,512]{3,2,1,0:T(8,128)}, f32[8,4,128,512]{3,2,1,0:T(8,128)S(1)}, u32[]{:S(2)}) %copy-start.2) | copy-done | bytes 8388632
  100.1 2.3 fusion.4
  102.5 16.1 %all-gather.19.cloned.1.call-done = bf16[1,8,512,192]{2,3,0,1:T(8,128)(2,1)} async-done(((bf16[1,8,128,192]{2,3,0,1:T(8,128)(2,1)}), bf16[1,8,512,192]{2,3,0,1:T(8,128)(2,1)}) %all-gather.19.cloned.1.call-update) | async-done | bytes 1572880 | tf_op jit(solution)/shard_map/all_gather | solution.py:117
  118.5 6.3 %fusion.56 = f32[8,128,4,48]{1,3,2,0:T(8,128)S(1)} fusion(bf16[8,512,4,48]{1,3,2,0:T(8,128)(2,1)} %bitcast.146, f32[8,4,128,512]{3,2,1,0:T(8,128)} %copy-done.2, f32[8,4,128]{2,1,0:T(4,128)S(1)} %broadcast_maximum_fusion.1, f32[4,128,512]{2,1,0:T(8,128)S(1)} %copy_bitcast_fusion.1, pred[512]{0:T(512)(128)(4,1)S(1)} %bitcast.142, f32[8,128,4]{1,2,0:T(4,128)S(1)} %bitcast.139), kind=kOutput, calls=%fused_computation.61 | convolution fusion | flops 212008960 | bytes 11829760 | tf_op jit(solution)/shard_map/shqk,skhd->shqd/dot_general | solution.py:103
  124.9 2.1 fusion.69
  127.1 18.2 %all-gather.13.cloned.1.call-done = bf16[8,128,768]{1,2,0:T(8,128)(2,1)} async-done(((bf16[8,128,192]{1,2,0:T(8,128)(2,1)}), bf16[8,128,768]{1,2,0:T(8,128)(2,1)}) %all-gather.13.cloned.1.call-update) | async-done | bytes 1572880 | tf_op jit(solution)/shard_map/all_gather | solution.py:132
  145.2 2.6 fusion.47
  147.9 19.8 %all-gather.15.cloned.1.call-done = bf16[8,128,768]{1,2,0:T(8,128)(2,1)} async-done(((bf16[8,128,192]{1,2,0:T(8,128)(2,1)}), bf16[8,128,768]{1,2,0:T(8,128)(2,1)}) %all-gather.15.cloned.1.call-update) | async-done | bytes 1572880 | tf_op jit(solution)/shard_map/all_gather | solution.py:71
  167.7 1.7 convert_reduce_fusion.1
  169.4 1.8 fusion.23
  171.3 4.4 %fusion.86 = (bf16[4,8,128,192]{2,3,0,1:T(8,128)(2,1)S(1)}, f32[4,8,128,192]{2,3,0,1:T(8,128)}) fusion(bf16[2,4,192,768]{3,2,1,0:T(8,128)(2,1)} %param.18, bf16[8,128,768]{1,2,0:T(8,128)(2,1)S(1)} %copy-done.6, f32[8,128]{1,0:T(8,128)S(1)} %add_rsqrt_fusion.1, f32[8,128]{1,0:T(8,128)S(1)} %broadcast_multiply_fusion.1), kind=kOutput, calls=%fused_computation.116 | convolution fusion | flops 1211891712 | bytes 7479296 | tf_op jit(solution)/shard_map/std,fed->fste/dot_general | solution.py:73
  175.7 1.2 copy-done.10
  177.8 1.5 collective-permute-start.3
  179.2 0.9 copy.29
  180.2 3.5 %all-to-all-start.1 = ((bf16[16,128,128]{2,1,0:T(8,128)(2,1)}), bf16[16,128,128]{2,1,0:T(8,128)(2,1)S(1)}, u32[]{:S(2)}, u32[]{:S(2)}) async-start(bf16[16,128,128]{2,1,0:T(8,128)(2,1)} %copy.29), calls=%async_computation.1 | async-start | bytes 1048576 | tf_op jit(solution)/shard_map/all_to_all | solution.py:70
  183.7 7.1 %collective-permute-done.3 = bf16[8,128,192]{1,2,0:T(8,128)(2,1)S(1)} collective-permute-done((bf16[8,128,192]{1,2,0:T(8,128)(2,1)S(1)}, bf16[8,128,192]{1,2,0:T(8,128)(2,1)S(1)}, u32[]{:S(2)}, u32[]{:S(2)}) %collective-permute-start.3) | collective-permute-done | bytes 393248 | tf_op jit(solution)/shard_map/ppermute | solution.py:19
  190.9 1.6 all-to-all-done.1
  192.6 10.5 %collective-permute-done.4 = bf16[8,128,192]{1,2,0:T(8,128)(2,1)S(1)} collective-permute-done((bf16[8,128,192]{1,2,0:T(8,128)(2,1)S(1)}, bf16[8,128,192]{1,2,0:T(8,128)(2,1)S(1)}, u32[]{:S(2)}, u32[]{:S(2)}) %collective-permute-start.4) | collective-permute-done | bytes 393248 | tf_op jit(solution)/shard_map/ppermute | solution.py:19
  203.2 1.1 constant_dynamic-update-slice_fusion.3
  204.6 19.9 %collective-permute-done.5 = bf16[8,128,192]{1,2,0:T(8,128)(2,1)S(1)} collective-permute-done((bf16[8,128,192]{1,2,0:T(8,128)(2,1)S(1)}, bf16[8,128,192]{1,2,0:T(8,128)(2,1)S(1)}, u32[]{:S(2)}, u32[]{:S(2)}) %collective-permute-start.5) | collective-permute-done | bytes 393248 | tf_op jit(solution)/shard_map/ppermute | solution.py:19
  224.6 1.9 fusion.9
  226.5 3.2 %copy-done.1 = f32[8,4,128,512]{3,2,1,0:T(8,128)} copy-done((f32[8,4,128,512]{3,2,1,0:T(8,128)}, f32[8,4,128,512]{3,2,1,0:T(8,128)S(1)}, u32[]{:S(2)}) %copy-start.1) | copy-done | bytes 8388632
  229.7 2.3 fusion.6
  232.1 5.5 %all-gather.21.cloned.1.call-done = bf16[1,8,512,192]{2,3,0,1:T(8,128)(2,1)} async-done(((bf16[1,8,128,192]{2,3,0,1:T(8,128)(2,1)}), bf16[1,8,512,192]{2,3,0,1:T(8,128)(2,1)}) %all-gather.21.cloned.1.call-update) | async-done | bytes 1572880 | tf_op jit(solution)/shard_map/all_gather | solution.py:117
  237.6 6.3 %fusion.53 = f32[8,128,4,48]{1,3,2,0:T(8,128)S(1)} fusion(bf16[8,512,4,48]{1,3,2,0:T(8,128)(2,1)} %bitcast.147, f32[8,4,128,512]{3,2,1,0:T(8,128)} %copy-done.1, f32[8,4,128]{2,1,0:T(4,128)S(1)} %broadcast_maximum_fusion, f32[4,128,512]{2,1,0:T(8,128)S(1)} %copy_bitcast_fusion, pred[512]{0:T(512)(128)(4,1)S(1)} %bitcast.145, f32[8,128,4]{1,2,0:T(4,128)S(1)} %bitcast.138), kind=kOutput, calls=%fused_computation.60 | convolution fusion | flops 212008960 | bytes 11829760 | tf_op jit(solution)/shard_map/shqk,skhd->shqd/dot_general | solution.py:103
  243.9 2.1 fusion.70
  246.0 18.0 %all-gather.17.cloned.1.call-done = bf16[8,128,768]{1,2,0:T(8,128)(2,1)} async-done(((bf16[8,128,192]{1,2,0:T(8,128)(2,1)}), bf16[8,128,768]{1,2,0:T(8,128)(2,1)}) %all-gather.17.cloned.1.call-update) | async-done | bytes 1572880 | tf_op jit(solution)/shard_map/all_gather | solution.py:132
  264.0 2.6 fusion.48
  (70 shorter events, 4.9 us)
Async XLA Ops:
  6.5 1.5 copy-start
  6.5 38.4 %all-gather.11.cloned.1.call-start = ((), (), s32[]{:S(2)}) async-start(), calls=%async_computation.2 | async-start | bytes 1966080 | tf_op jit(solution)/shard_map/all_gather | solution.py:71
  24.9 3.5 %copy-start.3 = (bf16[128,128,128]{2,1,0:T(8,128)(2,1)S(1)}, bf16[128,128,128]{2,1,0:T(8,128)(2,1)}, u32[]{:S(2)}) copy-start(bf16[128,128,128]{2,1,0:T(8,128)(2,1)} %param.11) | copy-start | bytes 12582916
  28.4 20.2 %copy-start.12 = (bf16[2,4,192,768]{3,2,1,0:T(8,128)(2,1)S(1)}, bf16[2,4,192,768]{3,2,1,0:T(8,128)(2,1)}, u32[]{:S(2)}) copy-start(bf16[2,4,192,768]{3,2,1,0:T(8,128)(2,1)} %param.18) | copy-start | bytes 7077892
  45.0 3.6 %copy-start.5 = (bf16[8,128,768]{1,2,0:T(8,128)(2,1)S(1)}, bf16[8,128,768]{1,2,0:T(8,128)(2,1)}, u32[]{:S(2)}) copy-start(bf16[8,128,768]{1,2,0:T(8,128)(2,1)} %all-gather.11.cloned.1.call-done) | copy-start | bytes 4718596
  48.6 5.6 %copy-start.4 = (bf16[128,128,128]{2,1,0:T(8,128)(2,1)S(1)}, bf16[128,128,128]{2,1,0:T(8,128)(2,1)}, u32[]{:S(2)}) copy-start(bf16[128,128,128]{2,1,0:T(8,128)(2,1)} %param.11) | copy-start | bytes 12582916
  48.6 5.6 %copy-start.13 = (bf16[128,2,16]{0,2,1:T(8,128)(2,1)S(1)}, bf16[128,2,16]{0,2,1:T(8,128)(2,1)}, u32[]{:S(2)}) copy-start(bf16[128,2,16]{0,2,1:T(8,128)(2,1)} %param.17) | copy-start | bytes 24580
  51.8 8.4 %copy-start.9 = (bf16[4,8,128,192]{2,3,0,1:T(8,128)(2,1)}, bf16[4,8,128,192]{2,3,0,1:T(8,128)(2,1)S(1)}, u32[]{:S(2)}) copy-start(bf16[4,8,128,192]{2,3,0,1:T(8,128)(2,1)S(1)} %get-tuple-element.15) | copy-start | bytes 4718596
  52.7 13.0 %collective-permute-start = (bf16[8,128,192]{1,2,0:T(8,128)(2,1)S(1)}, bf16[8,128,192]{1,2,0:T(8,128)(2,1)S(1)}, u32[]{:S(2)}, u32[]{:S(2)}) collective-permute-start(bf16[8,128,192]{1,2,0:T(8,128)(2,1)S(1)} %get-tuple-element.10), channel_id=1, source_target_pairs={{0,4},{4,8},{8,12},{12,0},{1,5},{5,9},{9,13},{13,1},{2,6},{6,10},{... | collective-permute-start | bytes 1179656 | tf_op jit(solution)/shard_map/ppermute | solution.py:19
  60.2 6.2 %copy-start.14 = (s32[128]{0:T(128)S(1)}, s32[128]{0:T(128)}, u32[]{:S(2)}) copy-start(s32[128]{0:T(128)} %param.12) | copy-start | bytes 1540
  61.4 20.0 %all-to-all-start = ((bf16[16,128,128]{2,1,0:T(8,128)(2,1)}), bf16[16,128,128]{2,1,0:T(8,128)(2,1)S(1)}, u32[]{:S(2)}, u32[]{:S(2)}) async-start(bf16[16,128,128]{2,1,0:T(8,128)(2,1)} %copy.26), calls=%async_computation | async-start | bytes 1048576 | tf_op jit(solution)/shard_map/all_to_all | solution.py:70
  64.8 53.7 %all-gather.19.cloned.1.call-start = ((), (), s32[]{:S(2)}) async-start(), calls=%async_computation.6 | async-start | bytes 1966080 | tf_op jit(solution)/shard_map/all_gather | solution.py:117
  65.8 15.7 %collective-permute-start.1 = (bf16[8,128,192]{1,2,0:T(8,128)(2,1)S(1)}, bf16[8,128,192]{1,2,0:T(8,128)(2,1)S(1)}, u32[]{:S(2)}, u32[]{:S(2)}) collective-permute-start(bf16[8,128,192]{1,2,0:T(8,128)(2,1)S(1)} %collective-permute-done), channel_id=1, source_target_pairs={{0,4},{4,8},{8,12},{12,0},{1,5},{5,9},{9,13},{13,1},{2,6},{6,10},{... | collective-permute-start | bytes 1179656 | tf_op jit(solution)/shard_map/ppermute | solution.py:19
  81.2 64.0 %all-gather.13.cloned.1.call-start = ((), (), s32[]{:S(2)}) async-start(), calls=%async_computation.3 | async-start | bytes 1966080 | tf_op jit(solution)/shard_map/all_gather | solution.py:132
  81.5 13.4 %collective-permute-start.2 = (bf16[8,128,192]{1,2,0:T(8,128)(2,1)S(1)}, bf16[8,128,192]{1,2,0:T(8,128)(2,1)S(1)}, u32[]{:S(2)}, u32[]{:S(2)}) collective-permute-start(bf16[8,128,192]{1,2,0:T(8,128)(2,1)S(1)} %collective-permute-done.1), channel_id=1, source_target_pairs={{0,4},{4,8},{8,12},{12,0},{1,5},{5,9},{9,13},{13,1},{2,6},{6,10},{... | collective-permute-start | bytes 1179656 | tf_op jit(solution)/shard_map/ppermute | solution.py:19
  96.9 3.2 %copy-start.2 = (f32[8,4,128,512]{3,2,1,0:T(8,128)}, f32[8,4,128,512]{3,2,1,0:T(8,128)S(1)}, u32[]{:S(2)}) copy-start(f32[8,4,128,512]{3,2,1,0:T(8,128)S(1)} %get-tuple-element.18) | copy-start | bytes 25165828
  118.5 26.7 %copy-start.7 = (bf16[8,128,192]{1,2,0:T(8,128)(2,1)S(1)}, bf16[8,128,192]{1,2,0:T(8,128)(2,1)}, u32[]{:S(2)}) copy-start(bf16[8,128,192]{1,2,0:T(8,128)(2,1)} %add_convert_fusion) | copy-start | bytes 1179652
  118.5 26.7 %copy-start.11 = (bf16[2,192,768]{2,1,0:T(8,128)(2,1)S(1)}, bf16[2,192,768]{2,1,0:T(8,128)(2,1)}, u32[]{:S(2)}) copy-start(bf16[2,192,768]{2,1,0:T(8,128)(2,1)} %param.19) | copy-start | bytes 1769476
  127.0 40.7 %all-gather.15.cloned.1.call-start = ((), (), s32[]{:S(2)}) async-start(), calls=%async_computation.4 | async-start | bytes 1966080 | tf_op jit(solution)/shard_map/all_gather | solution.py:71
  167.7 3.6 %copy-start.6 = (bf16[8,128,768]{1,2,0:T(8,128)(2,1)S(1)}, bf16[8,128,768]{1,2,0:T(8,128)(2,1)}, u32[]{:S(2)}) copy-start(bf16[8,128,768]{1,2,0:T(8,128)(2,1)} %all-gather.15.cloned.1.call-done) | copy-start | bytes 4718596
  175.7 1.2 copy-start.10
  177.8 13.0 %collective-permute-start.3 = (bf16[8,128,192]{1,2,0:T(8,128)(2,1)S(1)}, bf16[8,128,192]{1,2,0:T(8,128)(2,1)S(1)}, u32[]{:S(2)}, u32[]{:S(2)}) collective-permute-start(bf16[8,128,192]{1,2,0:T(8,128)(2,1)S(1)} %get-tuple-element.7), channel_id=1, source_target_pairs={{0,4},{4,8},{8,12},{12,0},{1,5},{5,9},{9,13},{13,1},{2,6},{6,10},{... | collective-permute-start | bytes 1179656 | tf_op jit(solution)/shard_map/ppermute | solution.py:19
  180.2 12.3 %all-to-all-start.1 = ((bf16[16,128,128]{2,1,0:T(8,128)(2,1)}), bf16[16,128,128]{2,1,0:T(8,128)(2,1)S(1)}, u32[]{:S(2)}, u32[]{:S(2)}) async-start(bf16[16,128,128]{2,1,0:T(8,128)(2,1)} %copy.29), calls=%async_computation.1 | async-start | bytes 1048576 | tf_op jit(solution)/shard_map/all_to_all | solution.py:70
  183.7 53.9 %all-gather.21.cloned.1.call-start = ((), (), s32[]{:S(2)}) async-start(), calls=%async_computation.7 | async-start | bytes 1966080 | tf_op jit(solution)/shard_map/all_gather | solution.py:117
  190.8 12.3 %collective-permute-start.4 = (bf16[8,128,192]{1,2,0:T(8,128)(2,1)S(1)}, bf16[8,128,192]{1,2,0:T(8,128)(2,1)S(1)}, u32[]{:S(2)}, u32[]{:S(2)}) collective-permute-start(bf16[8,128,192]{1,2,0:T(8,128)(2,1)S(1)} %collective-permute-done.3), channel_id=1, source_target_pairs={{0,4},{4,8},{8,12},{12,0},{1,5},{5,9},{9,13},{13,1},{2,6},{6,10},{... | collective-permute-start | bytes 1179656 | tf_op jit(solution)/shard_map/ppermute | solution.py:19
  190.8 73.2 %all-gather.17.cloned.1.call-start = ((), (), s32[]{:S(2)}) async-start(), calls=%async_computation.5 | async-start | bytes 1966080 | tf_op jit(solution)/shard_map/all_gather | solution.py:132
  203.1 21.4 %collective-permute-start.5 = (bf16[8,128,192]{1,2,0:T(8,128)(2,1)S(1)}, bf16[8,128,192]{1,2,0:T(8,128)(2,1)S(1)}, u32[]{:S(2)}, u32[]{:S(2)}) collective-permute-start(bf16[8,128,192]{1,2,0:T(8,128)(2,1)S(1)} %collective-permute-done.4), channel_id=1, source_target_pairs={{0,4},{4,8},{8,12},{12,0},{1,5},{5,9},{9,13},{13,1},{2,6},{6,10},{... | collective-permute-start | bytes 1179656 | tf_op jit(solution)/shard_map/ppermute | solution.py:19
  226.5 3.2 %copy-start.1 = (f32[8,4,128,512]{3,2,1,0:T(8,128)}, f32[8,4,128,512]{3,2,1,0:T(8,128)S(1)}, u32[]{:S(2)}) copy-start(f32[8,4,128,512]{3,2,1,0:T(8,128)S(1)} %get-tuple-element.22) | copy-start | bytes 25165828
  237.6 26.4 %copy-start.8 = (bf16[8,128,192]{1,2,0:T(8,128)(2,1)S(1)}, bf16[8,128,192]{1,2,0:T(8,128)(2,1)}, u32[]{:S(2)}) copy-start(bf16[8,128,192]{1,2,0:T(8,128)(2,1)} %fusion.47) | copy-start | bytes 1179652
Sparse Core Ops, SparseCore 0:
  25.0 19.9 all-gather.10
  81.3 37.1 all-gather.18
  127.1 18.0 all-gather.12
  148.0 19.6 all-gather.14
  191.0 46.5 all-gather.20
  246.2 17.8 all-gather.16
